TPU v7x, 512 devices: a whole 4x8x8 slice. The times are simulated.
512 devices in a mesh: occ: 16 (over z, y_lo), vir: 32 (over x, y_hi, core).
Axes of the slice: x: 4, y: 8 (y_hi: 4, y_lo: 2; y = y_hi * 2 + y_lo), z: 8, core: 2. Of those that a mesh axis runs over, the one named last changes fastest.
Arguments:
- amplitudes: float32 [32, 16, 256, 256], P('occ', None, 'vir'), may hold values from -6 to 6
- integrals: float32 [16, 256, 32, 256], P(None, 'occ', None, 'vir'), may hold values from -0.25 to 0.25
- tile_mask: int32 [32, 16, 4, 4], P('occ'), may hold values 0 or 1
- tile_irrep: int32 [36], replicated, may hold values from 0 to 7
Outputs:
- residual: float32 [32, 256, 32, 256], P('occ', 'vir')
All inputs are finite; a program needn't handle non-finite values. No bound on the sum of `tile_mask` on one device may be relied on, other than what follows from the above.
Results may differ from a plain program's by a relative error of at most 0.00007.
Values sent between devices are 32-bit elements; how exact they have to be, the bound alone decides.
A program may use at most 64 MiB of HBM per device.

v0:
```python
import jax
import jax.numpy as jnp
from jax import lax
from jax.sharding import PartitionSpec as P

NO = 32
V = 256
TILE = 64
KW = 16


def contract(amp_piece, int_piece):
    return jnp.einsum(
        "ikca,kcm->iam",
        amp_piece,
        int_piece,
        precision=lax.Precision.HIGHEST,
        preferred_element_type=jnp.float32,
    )


def body(amplitudes, integrals, tile_mask, tile_irrep):
    rows_own = amplitudes.shape[0]
    cols_own = integrals.shape[3]
    merged = NO * cols_own
    flat_int = integrals.reshape(integrals.shape[0], integrals.shape[1], merged)
    occ_label = tile_irrep[:NO]
    vir_label = jnp.repeat(tile_irrep[NO:], TILE)
    col_label = lax.dynamic_slice_in_dim(vir_label, lax.axis_index("vir") * cols_own, cols_own, 0)
    parity = jnp.bitwise_xor(
        jnp.bitwise_xor(occ_label[:KW, None, None, None], vir_label[None, :, None, None]),
        jnp.bitwise_xor(occ_label[None, None, :, None], col_label[None, None, None, :]),
    )
    symmetry = (parity == 0).astype(jnp.float32).reshape(KW, V, merged)
    kept = jnp.repeat(jnp.repeat(tile_mask, TILE, 2), TILE, 3).astype(jnp.float32)
    whole_int = lax.all_gather(flat_int, "occ", axis=1, tiled=True) * symmetry
    masked = lax.all_gather(amplitudes, "vir", axis=2, tiled=True) * kept
    flat_cycle = contract(masked, whole_int)
    local_cycle = flat_cycle.reshape(rows_own, V, NO, cols_own).transpose(0, 3, 2, 1)
    mirrored = lax.all_to_all(local_cycle, "occ", split_axis=2, concat_axis=0, tiled=True)
    return local_cycle - mirrored.transpose(2, 1, 0, 3)


def solution(mesh):
    return jax.shard_map(
        body,
        mesh=mesh,
        in_specs=(
            P("occ", None, "vir", None),
            P(None, "occ", None, "vir"),
            P("occ", None, None, None),
            P(),
        ),
        out_specs=P("occ", "vir", None, None),
        check_vma=False,
    )
```

profile of v0, /device:TPU:1, one launch (start us, length us, event | category | flops | bytes accessed | tf_op | source)
XLA Modules:
  0.0 257.2 jit_solution(15466749130097766590)
XLA Ops:
  6.5 0.0 all-gather.5.cloned.1.call-start
  6.5 2.0 copy.17
  8.5 1.3 copy.18
  9.8 0.0 all-gather.5.cloned.1.call-update
  9.9 0.0 all-gather.3.cloned.1.call-start
  9.9 0.8 copy.14
  10.7 0.0 all-gather.3.cloned.1.call-update
  10.7 0.0 copy-done.2
  10.8 0.1 copy.15
  10.9 0.2 broadcast_in_dim.12
  11.1 0.2 convert_element_type.14
  11.3 0.1 slice.11
  11.4 0.1 xor.61
  11.4 0.1 xor.62
  11.5 0.1 broadcast_in_dim.14
  11.6 0.1 xor.57
  11.7 0.1 dynamic_slice.3
  11.8 0.1 xor.64
  11.9 0.1 broadcast_xor_fusion
  12.0 106.7 %all-gather.5.cloned.1.call-done = f32[16,256,256]{2,0,1:T(8,128)} async-done(((f32[16,16,256]{2,0,1:T(8,128)}), f32[16,256,256]{2,0,1:T(8,128)}) %all-gather.5.cloned.1.call-update) | async-done | bytes 4194320 | tf_op jit(solution)/shard_map/all_gather | solution.py:36
  118.7 3.9 %fusion.2 = f32[16,256,256]{2,0,1:T(8,128)} fusion(f32[16,256,256]{2,0,1:T(8,128)} %all-gather.5.cloned.1.call-done, s32[256]{0:T(256)S(1)} %xor.65, s32[16,256]{0,1:T(8,128)S(1)} %broadcast_xor_fusion), kind=kLoop, calls=%fused_computation.4 | loop fusion | flops 3145728 | bytes 8406016 | tf_op jit(solution)/shard_map/mul | solution.py:36
  122.6 5.3 %copy.20 = f32[16,256,256]{1,2,0:T(8,128)} copy(f32[16,256,256]{2,0,1:T(8,128)} %fusion.2) | data formatting | bytes 8388608 | tf_op jit(solution)/shard_map/mul | solution.py:36
  127.9 73.2 %all-gather.3.cloned.1.call-done = f32[2,16,256,256]{3,1,0,2:T(8,128)} async-done(((f32[2,16,8,256]{3,1,0,2:T(8,128)}), f32[2,16,256,256]{3,1,0,2:T(8,128)}) %all-gather.3.cloned.1.call-update) | async-done | bytes 8388624 | tf_op jit(solution)/shard_map/all_gather | solution.py:37
  201.0 9.9 %copy.16 = f32[2,16,256,256]{2,3,1,0:T(8,128)} copy(f32[2,16,256,256]{3,1,0,2:T(8,128)} %all-gather.3.cloned.1.call-done) | data formatting | bytes 16777216 | tf_op jit(solution)/shard_map/all_gather | solution.py:37
  210.9 4.2 %bitcast_multiply_fusion = f32[2,16,256,256]{2,3,1,0:T(8,128)S(1)} fusion(f32[2,16,256,256]{2,3,1,0:T(8,128)} %copy.16, f32[2,16,256,4]{2,3,1,0:T(4,128)S(1)} %convert_element_type.14), kind=kLoop, calls=%fused_computation | loop fusion | flops 2097152 | bytes 16908288 | tf_op jit(solution)/shard_map/mul | solution.py:37
  215.2 0.3 copy-done
  215.5 7.7 %fusion.3 = f32[2,256,32,8]{1,3,2,0:T(8,128)S(1)} fusion(f32[2,16,256,256]{2,3,1,0:T(8,128)S(1)} %bitcast_multiply_fusion, f32[16,256,256]{1,2,0:T(8,128)S(1)} %copy-done), kind=kOutput, calls=%fused_computation.5 | convolution fusion | flops 6442450944 | bytes 13107200 | tf_op jit(solution)/shard_map/ikca,kcm->iam/dot_general | solution.py:13
  223.2 0.1 copy.29
  223.3 25.8 %all_to_all.18 = f32[2,8,32,256]{3,1,0,2:T(8,128)S(1)} all-to-all(f32[2,8,32,256]{3,1,0,2:T(8,128)S(1)} %bitcast.34), channel_id=1, replica_groups=mesh['occ'=16,'vir'=32] {'occ'}, dimensions={2} | all-to-all | bytes 1048576 | tf_op jit(solution)/shard_map/all_to_all | solution.py:40
  249.0 0.1 copy.22
  249.1 0.1 bitcast_subtract_fusion
  249.2 1.1 copy.23
  (9 shorter events, 0.0 us)
Async XLA Ops:
  6.5 3.4 %copy-start.1 = (f32[2,16,8,256]{3,2,1,0:T(8,128)S(1)}, f32[2,16,8,256]{3,2,1,0:T(8,128)}, u32[]{:S(2)}) copy-start(f32[2,16,8,256]{3,2,1,0:T(8,128)} %param.4) | copy-start | bytes 786436
  6.5 4.2 %copy-start.2 = (s32[2,16,4,4]{1,3,2,0:T(4,128)S(1)}, s32[2,16,4,4]{1,3,2,0:T(4,128)}, u32[]{:S(2)}) copy-start(s32[2,16,4,4]{1,3,2,0:T(4,128)} %param.6) | copy-start | bytes 6148
  6.5 4.7 %copy-start.3 = (s32[36]{0:T(128)S(1)}, s32[36]{0:T(128)}, u32[]{:S(2)}) copy-start(s32[36]{0:T(128)} %param.7) | copy-start | bytes 436
  6.5 112.2 %all-gather.5.cloned.1.call-start = ((), (), s32[]{:S(2)}) async-start(), calls=%async_computation.2 | async-start | bytes 4456448 | tf_op jit(solution)/shard_map/all_gather | solution.py:36
  9.9 191.2 %all-gather.3.cloned.1.call-start = ((), (), s32[]{:S(2)}) async-start(), calls=%async_computation.1 | async-start | bytes 8650752 | tf_op jit(solution)/shard_map/all_gather | solution.py:37
  210.9 4.6 %copy-start = (f32[16,256,256]{1,2,0:T(8,128)S(1)}, f32[16,256,256]{1,2,0:T(8,128)}, u32[]{:S(2)}) copy-start(f32[16,256,256]{1,2,0:T(8,128)} %copy.20) | copy-start | bytes 12582916
Sparse Core Ops, SparseCore 0:
  10.0 108.6 all-gather.4
  121.8 79.1 all-gather.2
where the time goes:
time: 259 us; the launch traced here: 257 us
  waiting for transfers between devices  180 us (69%)
  blocking collectives  25.8 us (10%)
  local copies, waits for them, and re-layouts  21.9 us (8%)
  between operations  13.5 us (5%)
  other arithmetic  8.31 us (3%)
  matrix products  7.69 us (3%)
    all_gather x1, waiting for transfers between devices, body(): whole_int = lax.all_gather(flat_int, 'occ', axis=1, tiled=True) * symmetry  107 us
    all_gather x1, waiting for transfers between devices, body(): masked = lax.all_gather(amplitudes, 'vir', axis=2, tiled=True) * kept  73.2 us
    all_to_all x1, blocking collectives, body(): lax.all_to_all(local_cycle, 'occ', split_axis=2, concat_axis=0, tiled=True)  25.8 us
    all_gather x1, local copies, waits for them, and re-layouts, body(): masked = lax.all_gather(amplitudes, 'vir', axis=2, tiled=True) * kept  9.89 us
    dot_general x1, matrix products, contract(): jnp.einsum('ikca,kcm->iam', amp_piece, int_piece, precision=lax.Precision...  7.69 us
    mul x1, local copies, waits for them, and re-layouts, body(): whole_int = lax.all_gather(flat_int, 'occ', axis=1, tiled=True) * symmetry  5.29 us
  transfers between devices with their start and end apart: 2, of which 2 were waited for; matrix products, arithmetic and copies ran while one was open for 4% of the time, Pallas kernels for 0%

commit v1 on v0

v1 whole, which is shorter than its diff:
```python
import jax
import jax.numpy as jnp
from jax import lax
from jax.experimental import pallas as pl
from jax.experimental.pallas import tpu as pltpu
from jax.sharding import PartitionSpec as P

NO = 32
V = 256
TILE = 64
KW = 16
MESH = pl.DeviceIdType.MESH
F32 = jnp.float32
BF16 = jnp.bfloat16


def split(value):
    high = value.astype(BF16)
    return high, (value - high.astype(F32)).astype(BF16)


def kernel(amp_ref, int_ref, mask_ref, irrep_ref, out_ref, amp_all, int_all, acc, cyc, mirror, send_sem, recv_sem, pass_send, pass_recv):
    occ, vir = lax.axis_index("occ"), lax.axis_index("vir")
    z, yl = occ // 2, occ % 2
    x, yh, core = vir // 8, (vir // 2) % 4, vir % 2

    def occ_at(dz, flip):
        return ((z + dz + 8) % 8) * 2 + (yl + flip) % 2

    def vir_at(dx, dy, flip):
        return (((x + dx + 4) % 4) * 4 + (yh + dy + 4) % 4) * 2 + (core + flip) % 2

    barrier = pltpu.get_barrier_semaphore()
    for step in range(1, 16):
        pl.semaphore_signal(barrier, inc=1, device_id=((occ + step) % 16, vir), device_id_type=MESH)
    for dx, dy, flip in ((1, 0, 0), (-1, 0, 0), (0, 1, 0), (0, -1, 0), (0, 0, 1)):
        pl.semaphore_signal(barrier, inc=1, device_id=(occ, vir_at(dx, dy, flip)), device_id_type=MESH)

    spread = (lax.broadcasted_iota(jnp.int32, (4, V), 1) // TILE == lax.broadcasted_iota(jnp.int32, (4, V), 0)).astype(F32)
    for i in range(2):
        kept = lax.dot_general(
            mask_ref[i, vir // 8].astype(F32), spread, (((0,), (0,)), ((), ())), preferred_element_type=F32
        )
        amp_all[i, vir] = amp_ref[i] * kept[:, None, :]

    lane = lax.broadcasted_iota(jnp.int32, (NO, V), 1) // 16
    row = lax.broadcasted_iota(jnp.int32, (NO, V), 0)
    label = jnp.full((NO, V), irrep_ref[NO + occ // 4] ^ irrep_ref[NO + vir // 8], jnp.int32)
    lanes = jnp.zeros((NO, V), jnp.int32)
    rows = jnp.zeros((NO, V), jnp.int32)
    for k in range(KW):
        lanes = jnp.where(lane == k, irrep_ref[k], lanes)
    for j in range(NO):
        rows = jnp.where(row == j, irrep_ref[j], rows)
    symmetry = ((label ^ lanes ^ rows) == 0).astype(F32)
    for b in range(8):
        int_all[occ, b * NO : (b + 1) * NO, :] = int_ref[pl.ds(b, V, stride=8), :].T * symmetry

    pl.semaphore_wait(barrier, 20)

    count = [0]
    sent = []

    def move(source, to, landing):
        slot = count[0]
        count[0] += 1
        copy = pltpu.make_async_remote_copy(
            src_ref=source, dst_ref=source, send_sem=send_sem.at[slot], recv_sem=recv_sem.at[slot], device_id=to, device_id_type=MESH
        )
        copy.start()
        sent.append(copy)
        arrival = pltpu.make_async_remote_copy(
            src_ref=landing, dst_ref=landing, send_sem=send_sem.at[slot], recv_sem=recv_sem.at[slot], device_id=to, device_id_type=MESH
        )
        return arrival.wait_recv

    arrivals = []
    x_wait = {}
    y_wait = {}
    z_wait = {}

    def block(i, dx, dy, flip=0):
        return amp_all.at[i, vir_at(dx, dy, flip)]

    def half(i, dx, dy, upper):
        return amp_all.at[i, vir_at(dx, dy, 0), pl.ds(8 * upper, 8)]

    right, left = (occ, vir_at(1, 0, 0)), (occ, vir_at(-1, 0, 0))
    up, down = (occ, vir_at(0, 1, 0)), (occ, vir_at(0, -1, 0))
    sibling = (occ, vir_at(0, 0, 1))

    def share(i, dx, dy):
        arrivals.append(move(block(i, dx, dy), sibling, block(i, dx, dy, 1)))

    def x_start(i, dy):
        x_wait[i, dy] = (
            move(block(i, 0, dy), right, block(i, -1, dy)),
            move(block(i, 0, dy), left, block(i, 1, dy)),
        )
        share(i, 0, dy)

    def x_forward(i, dy):
        first, second = x_wait[i, dy]
        first()
        one = move(half(i, -1, dy, 0), right, half(i, 2, dy, 0))
        share(i, -1, dy)
        second()
        two = move(half(i, 1, dy, 1), left, half(i, 2, dy, 1))
        share(i, 1, dy)
        x_wait[i, dy] = (one, two)

    def x_end(i, dy):
        one, two = x_wait[i, dy]
        one()
        two()
        share(i, 2, dy)

    def y_start(i):
        y_wait[i] = [move(block(i, 0, 0), up, block(i, 0, -1)), move(block(i, 0, 0), down, block(i, 0, 1))]

    def y_forward(i):
        first, second = y_wait[i]
        first()
        one = move(half(i, 0, -1, 0), up, half(i, 0, 2, 0))
        x_start(i, -1)
        second()
        two = move(half(i, 0, 1, 1), down, half(i, 0, 2, 1))
        x_start(i, 1)
        y_wait[i] = [one, two]

    def y_end(i):
        one, two = y_wait[i]
        one()
        two()
        x_start(i, 2)

    above, below = (occ_at(1, 0), vir), (occ_at(-1, 0), vir)

    def z_start(flip):
        z_wait[flip] = (
            move(int_all.at[occ_at(0, flip)], above, int_all.at[occ_at(-1, flip)]),
            move(int_all.at[occ_at(0, flip)], below, int_all.at[occ_at(1, flip)]),
        )

    def z_forward(flip, hop):
        first, second = z_wait[flip]
        first()
        if hop < 3:
            one = move(int_all.at[occ_at(-hop, flip)], above, int_all.at[occ_at(-hop - 1, flip)])
        else:
            one = move(int_all.at[occ_at(-3, flip), pl.ds(0, 128)], above, int_all.at[occ_at(4, flip), pl.ds(0, 128)])
        second()
        if hop < 3:
            two = move(int_all.at[occ_at(hop, flip)], below, int_all.at[occ_at(hop + 1, flip)])
        else:
            two = move(int_all.at[occ_at(3, flip), pl.ds(128, 128)], below, int_all.at[occ_at(4, flip), pl.ds(128, 128)])
        z_wait[flip] = (one, two)

    def z_end(flip):
        one, two = z_wait[flip]
        one()
        two()

    pair_wait = move(int_all.at[occ], (occ_at(0, 1), vir), int_all.at[occ_at(0, 1)])
    z_start(0)
    y_start(0)
    x_start(0, 0)
    y_start(1)
    x_start(1, 0)
    x_forward(0, 0)
    pair_wait()
    z_start(1)
    z_forward(0, 1)
    y_forward(0)
    x_forward(1, 0)
    y_forward(1)
    z_forward(1, 1)
    x_forward(0, -1)
    x_forward(0, 1)
    y_end(0)
    z_forward(0, 2)
    x_end(0, 0)
    x_end(1, 0)
    y_end(1)
    x_forward(1, -1)
    z_forward(1, 2)
    x_forward(1, 1)
    x_forward(0, 2)
    z_forward(0, 3)
    x_forward(1, 2)
    x_end(0, -1)
    x_end(0, 1)
    x_end(1, -1)
    x_end(1, 1)
    z_forward(1, 3)
    x_end(0, 2)
    x_end(1, 2)
    z_end(0)
    z_end(1)
    for wait in arrivals:
        wait()

    acc[...] = jnp.zeros_like(acc)

    def contract(o, carry):
        int_high, int_low = split(int_all[o])
        left_side = jnp.concatenate([int_high, int_high, int_low], axis=1)
        for i in range(2):
            piece = jnp.concatenate([amp_all[i, 2 * o][:, None], amp_all[i, 2 * o + 1][:, None]], axis=1).reshape(V, V)
            amp_high, amp_low = split(piece)
            right_side = jnp.concatenate([amp_high, amp_low, amp_high], axis=0)
            acc[i] += jnp.dot(left_side, right_side, preferred_element_type=F32)
        return carry

    lax.fori_loop(0, 16, contract, 0)

    for i in range(2):
        for b in range(8):
            for h in range(2):
                cyc[i, h, pl.ds(b, NO, stride=8), :] = acc[i, b * NO : (b + 1) * NO, h * 128 : (h + 1) * 128]
    passed = []
    for i in range(2):
        for step in range(1, 16):
            slot = i * 15 + step - 1
            to, origin = (occ + step) % 16, (occ + 16 - step) % 16
            copy = pltpu.make_async_remote_copy(
                src_ref=cyc.at[i, :, pl.ds(16 * to, 16)],
                dst_ref=mirror.at[:, pl.ds((2 * occ + i) * 16, 16)],
                send_sem=pass_send.at[slot],
                recv_sem=pass_recv.at[slot],
                device_id=(to, vir),
                device_id_type=MESH,
            )
            copy.start()
            landing = mirror.at[:, pl.ds((2 * origin + i) * 16, 16)]
            passed.append(
                (
                    copy,
                    pltpu.make_async_remote_copy(
                        src_ref=landing,
                        dst_ref=landing,
                        send_sem=pass_send.at[slot],
                        recv_sem=pass_recv.at[slot],
                        device_id=(to, vir),
                        device_id_type=MESH,
                    ),
                )
            )
        mirror[:, pl.ds((2 * occ + i) * 16, 16), :] = cyc[i, :, pl.ds(16 * occ, 16), :]
    for copy, arrival in passed:
        arrival.wait_recv()
    for i in range(2):
        for b in range(8):
            for h in range(2):
                out_ref[i, b, :, h * 128 : (h + 1) * 128] = (
                    acc[i, b * NO : (b + 1) * NO, h * 128 : (h + 1) * 128] - mirror[h, pl.ds(i * 8 + b, NO, stride=16), :]
                )
    for copy in sent:
        copy.wait_send()
    for copy, arrival in passed:
        copy.wait_send()


MOVES = 2 * (4 + 16 + 16) + 17


def body(amplitudes, integrals, tile_mask, tile_irrep):
    flat_int = integrals.transpose(0, 1, 3, 2).reshape(KW * 16 * 8, NO)
    mask = tile_mask.transpose(0, 2, 3, 1)
    vmem = pl.BlockSpec(memory_space=pltpu.VMEM)
    return pl.pallas_call(
        kernel,
        out_shape=jax.ShapeDtypeStruct((2, 8, NO, V), F32),
        in_specs=[vmem, vmem, vmem, pl.BlockSpec(memory_space=pltpu.SMEM)],
        out_specs=vmem,
        scratch_shapes=[
            pltpu.VMEM((2, 32, KW, 8, V), F32),
            pltpu.VMEM((16, V, V), F32),
            pltpu.VMEM((2, V, V), F32),
            pltpu.VMEM((2, 2, V, 128), F32),
            pltpu.VMEM((2, 2 * V, 128), F32),
            pltpu.SemaphoreType.DMA((MOVES,)),
            pltpu.SemaphoreType.DMA((MOVES,)),
            pltpu.SemaphoreType.DMA((30,)),
            pltpu.SemaphoreType.DMA((30,)),
        ],
        compiler_params=pltpu.CompilerParams(collective_id=0, has_side_effects=True, vmem_limit_bytes=48 << 20),
    )(amplitudes, flat_int, mask, tile_irrep)


def solution(mesh):
    return jax.shard_map(
        body,
        mesh=mesh,
        in_specs=(
            P("occ", None, "vir", None),
            P(None, "occ", None, "vir"),
            P("occ", None, None, None),
            P(),
        ),
        out_specs=P("occ", "vir", None, None),
        check_vma=False,
    )
```

time: 259 us -> 88.1 us (0.34)
  waiting for transfers between devices: 180 us -> 0 us
  Pallas kernels: 0 us -> 83 us
  blocking collectives: 25.8 us -> 0 us
  local copies, waits for them, and re-layouts: 21.9 us -> 4.34 us
  between operations: 13.5 us -> 0.01 us
  other arithmetic: 8.31 us -> 0 us
  matrix products: 7.69 us -> 0 us
    all_gather x2 -> x0, waiting for transfers between devices: 180 us -> none  [the longest x1 107 us: body(): whole_int = lax.all_gather(flat_int, 'occ', axis=1, tiled=True) * symmetry]
    pallas_call x0 -> x1, Pallas kernels: none -> 83 us  [body(): pl.pallas_call(kernel, out_shape=jax.ShapeDtypeStruct((2, 8, NO, V), F32)...]
    all_to_all x1 -> x0, blocking collectives: 25.8 us -> none  [body(): lax.all_to_all(local_cycle, 'occ', split_axis=2, concat_axis=0, tiled=True)]
    all_gather x1 -> x0, local copies, waits for them, and re-layouts: 9.89 us -> none  [body(): masked = lax.all_gather(amplitudes, 'vir', axis=2, tiled=True) * kept]
    mul x2 -> x0, other arithmetic: 8.11 us -> none  [the longest x1 4.24 us: body(): masked = lax.all_gather(amplitudes, 'vir', axis=2, tiled=True) * kept]
    dot_general x1 -> x0, matrix products: 7.69 us -> none  [contract(): jnp.einsum('ikca,kcm->iam', amp_piece, int_piece, precision=lax.Precision...]
    mul x1 -> x0, local copies, waits for them, and re-layouts: 5.29 us -> none  [body(): whole_int = lax.all_gather(flat_int, 'occ', axis=1, tiled=True) * symmetry]
  transfers between devices with their start and end apart: 2 -> 0, of which waited for: 2 -> 0; matrix products, arithmetic and copies ran while one was open for 4% -> 0% of each run, Pallas kernels for 0% -> 0%
where the time goes in v1:
time: 88.1 us; the launch traced here: 87.3 us
  Pallas kernels  83 us (94%)
  local copies, waits for them, and re-layouts  4.34 us (5%)
    pallas_call x1, Pallas kernels, body(): pl.pallas_call(kernel, out_shape=jax.ShapeDtypeStruct((2, 8, NO, V), F32)...  83 us
    unnamed x9, local copies, waits for them, and re-layouts  4.34 us

profile of v1, /device:TPU:1, one launch (start us, length us, event | category | flops | bytes accessed | tf_op | source)
XLA Modules:
  0.0 87.3 jit_solution(6851307866194744876)
XLA Ops:
  0.0 0.0 copy-start.3
  0.0 0.7 copy-done.3
  0.7 0.0 copy-start
  0.7 1.2 %copy-done = f32[16,16,32,8]{2,3,1,0:T(8,128)S(1)} copy-done((f32[16,16,32,8]{2,3,1,0:T(8,128)S(1)}, f32[16,16,32,8]{2,3,1,0:T(8,128)}, u32[]{:S(2)}) %copy-start) | copy-done | bytes 262168
  1.9 0.0 copy-start.1
  1.9 0.9 %copy-done.1 = f32[2,16,8,256]{3,2,1,0:T(8,128)S(1)} copy-done((f32[2,16,8,256]{3,2,1,0:T(8,128)S(1)}, f32[2,16,8,256]{3,2,1,0:T(8,128)}, u32[]{:S(2)}) %copy-start.1) | copy-done | bytes 262168
  2.8 0.0 copy-start.2
  2.8 0.7 copy-done.2
  3.5 83.0 %shard_map.46 = f32[2,8,32,256]{3,2,1,0:T(8,128)S(1)} custom-call(f32[2,16,8,256]{3,2,1,0:T(8,128)S(1)} %copy-done.1, f32[2048,32]{1,0:T(8,128)S(1)} %bitcast.4, s32[2,4,4,16]{3,2,1,0:T(4,128)S(1)} %bitcast.5, s32[36]{0:T(128)S(1)} %copy-done.3), custom_call_target="tpu_custom_call" | custom-call | tf_op jit(solution)/shard_map/pallas_call | solution.py:271
  86.5 0.8 copy.6
Async XLA Ops:
  0.0 0.7 copy-start.3
  0.7 1.2 %copy-start = (f32[16,16,32,8]{2,3,1,0:T(8,128)S(1)}, f32[16,16,32,8]{2,3,1,0:T(8,128)}, u32[]{:S(2)}) copy-start(f32[16,16,32,8]{2,3,1,0:T(8,128)} %param.5) | copy-start | bytes 786436
  1.9 0.9 %copy-start.1 = (f32[2,16,8,256]{3,2,1,0:T(8,128)S(1)}, f32[2,16,8,256]{3,2,1,0:T(8,128)}, u32[]{:S(2)}) copy-start(f32[2,16,8,256]{3,2,1,0:T(8,128)} %amp_ref.1) | copy-start | bytes 786436
  2.8 0.7 copy-start.2

commit v2 on v1

--- a/solution.py
+++ b/solution.py
@@ -9,6 +9,8 @@
 V = 256
 TILE = 64
 KW = 16
+DEPTH = 16
+FAR_FIRST = (8, 7, 9, 6, 10, 5, 11, 4, 12, 3, 13, 2, 14, 1, 15)
 MESH = pl.DeviceIdType.MESH
 F32 = jnp.float32
 BF16 = jnp.bfloat16
@@ -19,7 +21,7 @@
     return high, (value - high.astype(F32)).astype(BF16)
 
 
-def kernel(amp_ref, int_ref, mask_ref, irrep_ref, out_ref, amp_all, int_all, acc, cyc, mirror, send_sem, recv_sem, pass_send, pass_recv):
+def dense_kernel(amp_ref, int_ref, mask_ref, irrep_ref, out_ref, amp_all, int_all, acc, cyc, mirror, send_sem, recv_sem, pass_send, pass_recv):
     occ, vir = lax.axis_index("occ"), lax.axis_index("vir")
     z, yl = occ // 2, occ % 2
     x, yh, core = vir // 8, (vir // 2) % 4, vir % 2
@@ -261,15 +263,311 @@
         copy.wait_send()
 
 
+def sparse_kernel(
+    amp_hbm, int_hbm, mask_ref, irrep_ref, out_ref,
+    amp_in, int_in, turned, slots, amp_all, int_all, high_all, low_all, wide, acc, cyc, mirror,
+    in_sem, send_sem, recv_sem, pass_send, pass_recv,
+):
+    occ, vir = lax.axis_index("occ"), lax.axis_index("vir")
+    z, yl = occ // 2, occ % 2
+    x, yh, core = vir // 8, (vir // 2) % 4, vir % 2
+
+    def occ_at(dz, flip):
+        return ((z + dz + 8) % 8) * 2 + (yl + flip) % 2
+
+    def vir_at(dx, dy, flip):
+        return (((x + dx + 4) % 4) * 4 + (yh + dy + 4) % 4) * 2 + (core + flip) % 2
+
+    barrier = pltpu.get_barrier_semaphore()
+    for step in range(1, 16):
+        pl.semaphore_signal(barrier, inc=1, device_id=((occ + step) % 16, vir), device_id_type=MESH)
+    for dx, dy, flip in ((1, 0, 0), (-1, 0, 0), (0, 1, 0), (0, -1, 0), (0, 0, 1)):
+        pl.semaphore_signal(barrier, inc=1, device_id=(occ, vir_at(dx, dy, flip)), device_id_type=MESH)
+    load_int = pltpu.make_async_copy(int_hbm, int_in, in_sem.at[0])
+    load_amp = pltpu.make_async_copy(amp_hbm, amp_in, in_sem.at[1])
+    load_amp.start()
+    load_int.start()
+
+    lane = lax.broadcasted_iota(jnp.int32, (NO, V), 1) // 16
+    row = lax.broadcasted_iota(jnp.int32, (NO, V), 0)
+    labels = jnp.full((NO, V), irrep_ref[NO + vir // 8], jnp.int32)
+    for k in range(KW):
+        labels = jnp.where(lane == k, labels ^ irrep_ref[k], labels)
+    for j in range(NO):
+        labels = jnp.where(row == j, labels ^ irrep_ref[j], labels)
+    below = (lax.broadcasted_iota(jnp.int32, (NO, NO), 1) < lax.broadcasted_iota(jnp.int32, (NO, NO), 0)).astype(F32)
+    for tile in range(4):
+        allowed = (labels ^ irrep_ref[NO + tile]) == 0
+        rank = jnp.dot(below, allowed.astype(F32), preferred_element_type=F32)
+        slots[tile] = jnp.where(allowed, rank.astype(jnp.int32), -1)
+
+    spread = (lax.broadcasted_iota(jnp.int32, (4, V), 1) // TILE == lax.broadcasted_iota(jnp.int32, (4, V), 0)).astype(F32)
+    load_amp.wait()
+    for i in range(2):
+        kept = lax.dot_general(
+            mask_ref[i, vir // 8].astype(F32), spread, (((0,), (0,)), ((), ())), preferred_element_type=F32
+        )
+        amp_all[i, vir] = amp_in[i] * kept[:, None, :]
+
+    load_int.wait()
+    for b in range(8):
+        turned[b] = int_in[pl.ds(b, V, stride=8), :].T
+    depth = lax.broadcasted_iota(jnp.int32, (DEPTH, V), 0)
+
+    def pack(b, carry):
+        packed = jnp.zeros((DEPTH, V), F32)
+        for j in range(NO):
+            place = jnp.broadcast_to(slots[occ // 4, j : j + 1, :], (DEPTH, V))
+            packed = jnp.where(place == depth, jnp.broadcast_to(turned[b, j : j + 1, :], (DEPTH, V)), packed)
+        int_all[occ, b] = packed
+        return carry
+
+    lax.fori_loop(0, 8, pack, 0)
+    pl.semaphore_wait(barrier, 20)
+
+    count = [0]
+    sent = []
+
+    def move(source, to, landing):
+        slot = count[0]
+        count[0] += 1
+        copy = pltpu.make_async_remote_copy(
+            src_ref=source, dst_ref=source, send_sem=send_sem.at[slot], recv_sem=recv_sem.at[slot], device_id=to, device_id_type=MESH
+        )
+        copy.start()
+        sent.append(copy)
+        arrival = pltpu.make_async_remote_copy(
+            src_ref=landing, dst_ref=landing, send_sem=send_sem.at[slot], recv_sem=recv_sem.at[slot], device_id=to, device_id_type=MESH
+        )
+        return arrival.wait_recv
+
+    share_wait = {}
+    x_wait = {}
+    y_wait = {}
+    z_wait = {}
+
+    def block(i, dx, dy, flip=0):
+        return amp_all.at[i, vir_at(dx, dy, flip)]
+
+    def half(i, dx, dy, upper):
+        return amp_all.at[i, vir_at(dx, dy, 0), pl.ds(8 * upper, 8)]
+
+    right, left = (occ, vir_at(1, 0, 0)), (occ, vir_at(-1, 0, 0))
+    up, down = (occ, vir_at(0, 1, 0)), (occ, vir_at(0, -1, 0))
+    sibling = (occ, vir_at(0, 0, 1))
+
+    def share(i, dx, dy):
+        share_wait[i, dx, dy] = move(block(i, dx, dy), sibling, block(i, dx, dy, 1))
+
+    def x_start(i, dy):
+        x_wait[i, dy] = (
+            move(block(i, 0, dy), right, block(i, -1, dy)),
+            move(block(i, 0, dy), left, block(i, 1, dy)),
+        )
+        share(i, 0, dy)
+
+    def x_forward(i, dy):
+        first, second = x_wait[i, dy]
+        first()
+        one = move(half(i, -1, dy, 0), right, half(i, 2, dy, 0))
+        share(i, -1, dy)
+        second()
+        two = move(half(i, 1, dy, 1), left, half(i, 2, dy, 1))
+        share(i, 1, dy)
+        x_wait[i, dy] = (one, two)
+
+    def x_end(i, dy):
+        one, two = x_wait[i, dy]
+        one()
+        two()
+        share(i, 2, dy)
+
+    def y_start(i):
+        y_wait[i] = [move(block(i, 0, 0), up, block(i, 0, -1)), move(block(i, 0, 0), down, block(i, 0, 1))]
+
+    def y_forward(i):
+        first, second = y_wait[i]
+        first()
+        one = move(half(i, 0, -1, 0), up, half(i, 0, 2, 0))
+        x_start(i, -1)
+        second()
+        two = move(half(i, 0, 1, 1), down, half(i, 0, 2, 1))
+        x_start(i, 1)
+        y_wait[i] = [one, two]
+
+    def y_end(i):
+        one, two = y_wait[i]
+        one()
+        two()
+        x_start(i, 2)
+
+    above, below_z = (occ_at(1, 0), vir), (occ_at(-1, 0), vir)
+
+    def z_start(flip):
+        z_wait[flip] = (
+            move(int_all.at[occ_at(0, flip)], above, int_all.at[occ_at(-1, flip)]),
+            move(int_all.at[occ_at(0, flip)], below_z, int_all.at[occ_at(1, flip)]),
+        )
+
+    def z_forward(flip, hop):
+        first, second = z_wait[flip]
+        first()
+        if hop < 3:
+            one = move(int_all.at[occ_at(-hop, flip)], above, int_all.at[occ_at(-hop - 1, flip)])
+        else:
+            one = move(int_all.at[occ_at(-3, flip), pl.ds(0, 4)], above, int_all.at[occ_at(4, flip), pl.ds(0, 4)])
+        second()
+        if hop < 3:
+            two = move(int_all.at[occ_at(hop, flip)], below_z, int_all.at[occ_at(hop + 1, flip)])
+        else:
+            two = move(int_all.at[occ_at(3, flip), pl.ds(4, 4)], below_z, int_all.at[occ_at(4, flip), pl.ds(4, 4)])
+        z_wait[flip] = (one, two)
+
+    def z_end(flip):
+        one, two = z_wait[flip]
+        one()
+        two()
+
+    def unpack(*places):
+        for dz, flip in places:
+            o = occ_at(dz, flip)
+
+            def one(b, carry, o=o):
+                for g in range(4):
+                    for h in range(2):
+                        cols = pl.ds(128 * h, 128)
+                        place = slots[o // 4, 8 * g : 8 * g + 8, cols]
+                        near = jnp.take_along_axis(int_all[o, b, 0:8, cols], place & 7, axis=0)
+                        far = jnp.take_along_axis(int_all[o, b, 8:16, cols], place & 7, axis=0)
+                        value = jnp.where(place < 0, 0.0, jnp.where(place < 8, near, far))
+                        wide[pl.ds(b * NO + 8 * g, 8), cols] = value
+                return carry
+
+            lax.fori_loop(0, 8, one, 0)
+            high_all[o], low_all[o] = split(wide[...])
+
+    def contract(i, dx, start=False):
+        base = ((x + dx + 4) % 4) * 4
+
+        def one(step, carry):
+            o = base + step
+            high = high_all[o]
+            left_side = jnp.concatenate([high, high, low_all[o]], axis=1)
+            piece = jnp.concatenate([amp_all[i, 2 * o][:, None], amp_all[i, 2 * o + 1][:, None]], axis=1).reshape(V, V)
+            amp_high, amp_low = split(piece)
+            right_side = jnp.concatenate([amp_high, amp_low, amp_high], axis=0)
+            acc[i] += jnp.dot(left_side, right_side, preferred_element_type=F32)
+            return carry
+
+        for dy in (0, -1, 1, 2):
+            share_wait[i, dx, dy]()
+        if start:
+            acc[i] = jnp.zeros((V, V), F32)
+        lax.fori_loop(0, 4, one, 0)
+
+    passed = []
+
+    def exchange(i):
+        for b in range(8):
+            for h in range(2):
+                cyc[i, h, pl.ds(b, NO, stride=8), :] = acc[i, b * NO : (b + 1) * NO, h * 128 : (h + 1) * 128]
+        for step in FAR_FIRST:
+            slot = i * 15 + step - 1
+            to, origin = (occ + step) % 16, (occ + 16 - step) % 16
+            copy = pltpu.make_async_remote_copy(
+                src_ref=cyc.at[i, :, pl.ds(16 * to, 16)],
+                dst_ref=mirror.at[:, pl.ds((2 * occ + i) * 16, 16)],
+                send_sem=pass_send.at[slot],
+                recv_sem=pass_recv.at[slot],
+                device_id=(to, vir),
+                device_id_type=MESH,
+            )
+            copy.start()
+            landing = mirror.at[:, pl.ds((2 * origin + i) * 16, 16)]
+            arrival = pltpu.make_async_remote_copy(
+                src_ref=landing,
+                dst_ref=landing,
+                send_sem=pass_send.at[slot],
+                recv_sem=pass_recv.at[slot],
+                device_id=(to, vir),
+                device_id_type=MESH,
+            )
+            passed.append((copy, arrival))
+        mirror[:, pl.ds((2 * occ + i) * 16, 16), :] = cyc[i, :, pl.ds(16 * occ, 16), :]
+
+    y_start(0)
+    x_start(0, 0)
+    z_start(0)
+    pair_wait = move(int_all.at[occ], (occ_at(0, 1), vir), int_all.at[occ_at(0, 1)])
+    x_start(1, 0)
+    unpack((0, 0))
+    x_forward(0, 0)
+    z_forward(0, 1)
+    y_forward(0)
+    y_start(1)
+    z_forward(0, 2)
+    x_end(0, 0)
+    pair_wait()
+    z_start(1)
+    z_forward(0, 3)
+    x_forward(0, -1)
+    y_end(0)
+    unpack((1, 0), (-1, 0))
+    z_forward(1, 1)
+    x_forward(0, 1)
+    z_end(0)
+    unpack((2, 0), (-2, 0))
+    x_forward(1, 0)
+    z_forward(1, 2)
+    x_forward(0, 2)
+    y_forward(1)
+    unpack((3, 0), (-3, 0))
+    z_forward(1, 3)
+    y_end(1)
+    x_end(0, -1)
+    x_end(0, 1)
+    unpack((4, 0), (0, 1), (1, 1), (-1, 1))
+    x_end(0, 2)
+    x_end(1, 0)
+    z_end(1)
+    unpack((2, 1), (-2, 1), (3, 1), (-3, 1), (4, 1))
+    contract(0, 0, True)
+    contract(0, 1)
+    contract(0, -1)
+    contract(0, 2)
+    exchange(0)
+    x_forward(1, -1)
+    contract(1, 0, True)
+    x_forward(1, 1)
+    x_forward(1, 2)
+    contract(1, 1)
+    contract(1, -1)
+    x_end(1, -1)
+    x_end(1, 1)
+    x_end(1, 2)
+    contract(1, 2)
+    exchange(1)
+    for copy in sent:
+        copy.wait_send()
+    for copy, arrival in passed:
+        arrival.wait_recv()
+    for i in range(2):
+        for b in range(8):
+            for h in range(2):
+                out_ref[i, b, :, h * 128 : (h + 1) * 128] = (
+                    acc[i, b * NO : (b + 1) * NO, h * 128 : (h + 1) * 128] - mirror[h, pl.ds(i * 8 + b, NO, stride=16), :]
+                )
+    for copy, arrival in passed:
+        copy.wait_send()
+
+
 MOVES = 2 * (4 + 16 + 16) + 17
 
 
-def body(amplitudes, integrals, tile_mask, tile_irrep):
-    flat_int = integrals.transpose(0, 1, 3, 2).reshape(KW * 16 * 8, NO)
-    mask = tile_mask.transpose(0, 2, 3, 1)
+def dense(amplitudes, flat_int, mask, tile_irrep):
     vmem = pl.BlockSpec(memory_space=pltpu.VMEM)
     return pl.pallas_call(
-        kernel,
+        dense_kernel,
         out_shape=jax.ShapeDtypeStruct((2, 8, NO, V), F32),
         in_specs=[vmem, vmem, vmem, pl.BlockSpec(memory_space=pltpu.SMEM)],
         out_specs=vmem,
@@ -288,6 +586,45 @@
     )(amplitudes, flat_int, mask, tile_irrep)
 
 
+def sparse(amplitudes, flat_int, mask, tile_irrep):
+    vmem = pl.BlockSpec(memory_space=pltpu.VMEM)
+    hbm = pl.BlockSpec(memory_space=pl.ANY)
+    return pl.pallas_call(
+        sparse_kernel,
+        out_shape=jax.ShapeDtypeStruct((2, 8, NO, V), F32),
+        in_specs=[hbm, hbm, vmem, pl.BlockSpec(memory_space=pltpu.SMEM)],
+        out_specs=vmem,
+        scratch_shapes=[
+            pltpu.VMEM((2, KW, 8, V), F32),
+            pltpu.VMEM((KW * 16 * 8, NO), F32),
+            pltpu.VMEM((8, NO, V), F32),
+            pltpu.VMEM((4, NO, V), jnp.int32),
+            pltpu.VMEM((2, 32, KW, 8, V), F32),
+            pltpu.VMEM((16, 8, DEPTH, V), F32),
+            pltpu.VMEM((16, V, V), BF16),
+            pltpu.VMEM((16, V, V), BF16),
+            pltpu.VMEM((V, V), F32),
+            pltpu.VMEM((2, V, V), F32),
+            pltpu.VMEM((2, 2, V, 128), F32),
+            pltpu.VMEM((2, 2 * V, 128), F32),
+            pltpu.SemaphoreType.DMA((2,)),
+            pltpu.SemaphoreType.DMA((MOVES,)),
+            pltpu.SemaphoreType.DMA((MOVES,)),
+            pltpu.SemaphoreType.DMA((30,)),
+            pltpu.SemaphoreType.DMA((30,)),
+        ],
+        compiler_params=pltpu.CompilerParams(collective_id=1, has_side_effects=True, vmem_limit_bytes=56 << 20),
+    )(amplitudes, flat_int, mask, tile_irrep)
+
+
+def body(amplitudes, integrals, tile_mask, tile_irrep):
+    flat_int = integrals.transpose(0, 1, 3, 2).reshape(KW * 16 * 8, NO)
+    mask = tile_mask.transpose(0, 2, 3, 1)
+    occupied = tile_irrep[:NO]
+    largest = jnp.max(jnp.sum((occupied[:, None] == occupied[None, :]).astype(jnp.int32), axis=1))
+    return lax.cond(largest <= DEPTH, sparse, dense, amplitudes, flat_int, mask, tile_irrep)
+
+
 def solution(mesh):
     return jax.shard_map(
         body,

time: 88.1 us -> 74.6 us (0.85)
  Pallas kernels: 83 us -> 71.5 us
  local copies, waits for them, and re-layouts: 4.34 us -> 1.45 us
    pallas_call x1, Pallas kernels: 83 us -> 71.5 us  [sparse(): pl.pallas_call(sparse_kernel, out_shape=jax.ShapeDtypeStruct((2, 8, NO, V...]
    unnamed x9 -> x3, local copies, waits for them, and re-layouts: 4.34 us -> 1.45 us
where the time goes in v2:
time: 74.6 us; the launch traced here: 74.4 us
  Pallas kernels  71.5 us (96%)
  local copies, waits for them, and re-layouts  1.45 us (2%)
  other arithmetic  0.82 us (1%)
    pallas_call x1, Pallas kernels, sparse(): pl.pallas_call(sparse_kernel, out_shape=jax.ShapeDtypeStruct((2, 8, NO, V...  71.5 us

profile of v2, /device:TPU:1, one launch (start us, length us, event | category | flops | bytes accessed | tf_op | source)
XLA Modules:
  0.0 74.4 jit_solution(5058910614502014921)
XLA Ops:
  0.0 0.0 copy-start
  0.0 0.7 copy-done
  0.7 0.2 convert_reduce_fusion
  0.8 0.6 reduce_max.9
  2.1 71.5 %conditional.1 = (f32[2,8,32,256]{3,2,1,0:T(8,128)S(1)}) conditional(s32[]{:T(128)} %convert_element_type.7, (f32[2,16,8,256]{3,2,1,0:T(8,128)}, f32[16,16,8,32]{3,2,1,0:T(8,128)}, s32[2,4,4,16]{3,2,1,0:T(4,128)}, s32[36]{0:T(128)S(1)}) %tuple.20, (f32[2,16,8,256]{3,2,1,0:T(8,128)}, f32[16,16,8,32]{3,2,1,0:T(8,128)}, s32[2,4,4,16]{3,2,1,0:T(4,128)}, ...), branch_computations={%region_2.0_spmd, %region_3.0_spmd} | conditional | bytes 8 | solution.py:625
  2.1 71.5 %branch_1_fun.1 = f32[2,8,32,256]{3,2,1,0:T(8,128)S(1)} custom-call(f32[2,16,8,256]{3,2,1,0:T(8,128)} %get-tuple-element.38.amp_hbm, f32[2048,32]{1,0:T(8,128)} %bitcast.8, s32[2,4,4,16]{3,2,1,0:T(4,128)} %get-tuple-element.30.mask_ref, s32[36]{0:T(128)S(1)} %get-tuple-element.31.irrep_ref), custom_call_target="tpu_custom_call" | custom-call | tf_op jit(solution)/shard_map/cond/branch_1_fun/pallas_call | solution.py:592
  73.6 0.8 %copy.12 = f32[2,8,32,256]{3,2,1,0:T(8,128)} copy(f32[2,8,32,256]{3,2,1,0:T(8,128)S(1)} %get-tuple-element.32) | data formatting | bytes 1048576
Async XLA Ops:
  0.0 0.7 copy-start

commit v3 on v2

--- a/solution.py
+++ b/solution.py
@@ -288,19 +288,6 @@
     load_amp.start()
     load_int.start()
 
-    lane = lax.broadcasted_iota(jnp.int32, (NO, V), 1) // 16
-    row = lax.broadcasted_iota(jnp.int32, (NO, V), 0)
-    labels = jnp.full((NO, V), irrep_ref[NO + vir // 8], jnp.int32)
-    for k in range(KW):
-        labels = jnp.where(lane == k, labels ^ irrep_ref[k], labels)
-    for j in range(NO):
-        labels = jnp.where(row == j, labels ^ irrep_ref[j], labels)
-    below = (lax.broadcasted_iota(jnp.int32, (NO, NO), 1) < lax.broadcasted_iota(jnp.int32, (NO, NO), 0)).astype(F32)
-    for tile in range(4):
-        allowed = (labels ^ irrep_ref[NO + tile]) == 0
-        rank = jnp.dot(below, allowed.astype(F32), preferred_element_type=F32)
-        slots[tile] = jnp.where(allowed, rank.astype(jnp.int32), -1)
-
     spread = (lax.broadcasted_iota(jnp.int32, (4, V), 1) // TILE == lax.broadcasted_iota(jnp.int32, (4, V), 0)).astype(F32)
     load_amp.wait()
     for i in range(2):
@@ -309,20 +296,6 @@
         )
         amp_all[i, vir] = amp_in[i] * kept[:, None, :]
 
-    load_int.wait()
-    for b in range(8):
-        turned[b] = int_in[pl.ds(b, V, stride=8), :].T
-    depth = lax.broadcasted_iota(jnp.int32, (DEPTH, V), 0)
-
-    def pack(b, carry):
-        packed = jnp.zeros((DEPTH, V), F32)
-        for j in range(NO):
-            place = jnp.broadcast_to(slots[occ // 4, j : j + 1, :], (DEPTH, V))
-            packed = jnp.where(place == depth, jnp.broadcast_to(turned[b, j : j + 1, :], (DEPTH, V)), packed)
-        int_all[occ, b] = packed
-        return carry
-
-    lax.fori_loop(0, 8, pack, 0)
     pl.semaphore_wait(barrier, 20)
 
     count = [0]
@@ -403,30 +376,36 @@
 
     above, below_z = (occ_at(1, 0), vir), (occ_at(-1, 0), vir)
 
-    def z_start(flip):
-        z_wait[flip] = (
-            move(int_all.at[occ_at(0, flip)], above, int_all.at[occ_at(-1, flip)]),
-            move(int_all.at[occ_at(0, flip)], below_z, int_all.at[occ_at(1, flip)]),
-        )
-
-    def z_forward(flip, hop):
-        first, second = z_wait[flip]
+    def piece(dz, flip, part):
+        return int_all.at[occ_at(dz, flip), pl.ds(4 * part, 4)]
+
+    def z_start(flip, part):
+        z_wait[flip, part] = [
+            move(piece(0, flip, part), above, piece(-1, flip, part)),
+            move(piece(0, flip, part), below_z, piece(1, flip, part)),
+        ]
+
+    def z_forward(flip, hop, part):
+        first, second = z_wait[flip, part]
+        onward = []
         first()
-        if hop < 3:
-            one = move(int_all.at[occ_at(-hop, flip)], above, int_all.at[occ_at(-hop - 1, flip)])
-        else:
-            one = move(int_all.at[occ_at(-3, flip), pl.ds(0, 4)], above, int_all.at[occ_at(4, flip), pl.ds(0, 4)])
+        if hop < 3 or part == 0:
+            onward.append(move(piece(-hop, flip, part), above, piece(-hop - 1, flip, part)))
         second()
-        if hop < 3:
-            two = move(int_all.at[occ_at(hop, flip)], below_z, int_all.at[occ_at(hop + 1, flip)])
-        else:
-            two = move(int_all.at[occ_at(3, flip), pl.ds(4, 4)], below_z, int_all.at[occ_at(4, flip), pl.ds(4, 4)])
-        z_wait[flip] = (one, two)
-
-    def z_end(flip):
-        one, two = z_wait[flip]
-        one()
-        two()
+        if hop < 3 or part == 1:
+            onward.append(move(piece(hop, flip, part), below_z, piece(hop + 1, flip, part)))
+        z_wait[flip, part] = onward
+
+    def z_end(flip, part):
+        for wait in z_wait[flip, part]:
+            wait()
+
+    def pair_start(part):
+        z_wait["pair", part] = move(piece(0, 0, part), (occ_at(0, 1), vir), piece(0, 1, part))
+
+    def pair_end(part):
+        z_wait["pair", part]()
+        z_start(1, part)
 
     def unpack(*places):
         for dz, flip in places:
@@ -497,53 +476,91 @@
 
     y_start(0)
     x_start(0, 0)
-    z_start(0)
-    pair_wait = move(int_all.at[occ], (occ_at(0, 1), vir), int_all.at[occ_at(0, 1)])
     x_start(1, 0)
+
+    lane = lax.broadcasted_iota(jnp.int32, (NO, V), 1) // 16
+    row = lax.broadcasted_iota(jnp.int32, (NO, V), 0)
+    labels = jnp.full((NO, V), irrep_ref[NO + vir // 8], jnp.int32)
+    for k in range(KW):
+        labels = jnp.where(lane == k, labels ^ irrep_ref[k], labels)
+    for j in range(NO):
+        labels = jnp.where(row == j, labels ^ irrep_ref[j], labels)
+    below = (lax.broadcasted_iota(jnp.int32, (NO, NO), 1) < lax.broadcasted_iota(jnp.int32, (NO, NO), 0)).astype(F32)
+    for tile in range(4):
+        allowed = (labels ^ irrep_ref[NO + tile]) == 0
+        rank = jnp.dot(below, allowed.astype(F32), preferred_element_type=F32)
+        slots[tile] = jnp.where(allowed, rank.astype(jnp.int32), -1)
+
+    load_int.wait()
+    for b in range(8):
+        turned[b] = int_in[pl.ds(b, V, stride=8), :].T
+    depth = lax.broadcasted_iota(jnp.int32, (DEPTH, V), 0)
+
+    def pack(b, carry):
+        packed = jnp.zeros((DEPTH, V), F32)
+        for j in range(NO):
+            place = jnp.broadcast_to(slots[occ // 4, j : j + 1, :], (DEPTH, V))
+            packed = jnp.where(place == depth, jnp.broadcast_to(turned[b, j : j + 1, :], (DEPTH, V)), packed)
+        int_all[occ, b] = packed
+        return carry
+
+    lax.fori_loop(0, 8, pack, 0)
+    z_start(0, 0)
+    z_start(0, 1)
+    pair_start(0)
+    pair_start(1)
     unpack((0, 0))
+    z_forward(0, 1, 0)
     x_forward(0, 0)
-    z_forward(0, 1)
+    z_forward(0, 1, 1)
+    z_forward(0, 2, 0)
     y_forward(0)
     y_start(1)
-    z_forward(0, 2)
+    z_forward(0, 2, 1)
     x_end(0, 0)
-    pair_wait()
-    z_start(1)
-    z_forward(0, 3)
+    pair_end(0)
+    z_forward(0, 3, 0)
+    pair_end(1)
+    z_forward(0, 3, 1)
     x_forward(0, -1)
+    z_forward(1, 1, 0)
     y_end(0)
-    unpack((1, 0), (-1, 0))
-    z_forward(1, 1)
+    z_forward(1, 1, 1)
+    z_end(0, 0)
+    z_end(0, 1)
+    unpack((1, 0), (-1, 0), (2, 0), (-2, 0))
     x_forward(0, 1)
-    z_end(0)
-    unpack((2, 0), (-2, 0))
+    z_forward(1, 2, 0)
+    unpack((3, 0), (-3, 0), (4, 0), (0, 1))
     x_forward(1, 0)
-    z_forward(1, 2)
+    z_forward(1, 2, 1)
+    y_forward(1)
+    z_forward(1, 3, 0)
     x_forward(0, 2)
-    y_forward(1)
-    unpack((3, 0), (-3, 0))
-    z_forward(1, 3)
-    y_end(1)
+    z_forward(1, 3, 1)
+    unpack((1, 1), (-1, 1), (2, 1), (-2, 1))
     x_end(0, -1)
     x_end(0, 1)
-    unpack((4, 0), (0, 1), (1, 1), (-1, 1))
+    unpack((3, 1), (-3, 1))
+    z_end(1, 0)
+    z_end(1, 1)
+    unpack((4, 1))
+    contract(0, 0, True)
+    y_end(1)
     x_end(0, 2)
-    x_end(1, 0)
-    z_end(1)
-    unpack((2, 1), (-2, 1), (3, 1), (-3, 1), (4, 1))
-    contract(0, 0, True)
     contract(0, 1)
     contract(0, -1)
+    x_forward(1, -1)
     contract(0, 2)
     exchange(0)
-    x_forward(1, -1)
+    x_end(1, 0)
+    x_forward(1, 1)
     contract(1, 0, True)
-    x_forward(1, 1)
     x_forward(1, 2)
+    x_end(1, -1)
     contract(1, 1)
+    x_end(1, 1)
     contract(1, -1)
-    x_end(1, -1)
-    x_end(1, 1)
     x_end(1, 2)
     contract(1, 2)
     exchange(1)
@@ -608,8 +625,8 @@
             pltpu.VMEM((2, 2, V, 128), F32),
             pltpu.VMEM((2, 2 * V, 128), F32),
             pltpu.SemaphoreType.DMA((2,)),
-            pltpu.SemaphoreType.DMA((MOVES,)),
-            pltpu.SemaphoreType.DMA((MOVES,)),
+            pltpu.SemaphoreType.DMA((MOVES + 13,)),
+            pltpu.SemaphoreType.DMA((MOVES + 13,)),
             pltpu.SemaphoreType.DMA((30,)),
             pltpu.SemaphoreType.DMA((30,)),
         ],
@@ -621,8 +638,8 @@
     flat_int = integrals.transpose(0, 1, 3, 2).reshape(KW * 16 * 8, NO)
     mask = tile_mask.transpose(0, 2, 3, 1)
     occupied = tile_irrep[:NO]
-    largest = jnp.max(jnp.sum((occupied[:, None] == occupied[None, :]).astype(jnp.int32), axis=1))
-    return lax.cond(largest <= DEPTH, sparse, dense, amplitudes, flat_int, mask, tile_irrep)
+    pairs = jnp.sum((occupied[:, None] == occupied[None, :]).astype(jnp.int32))
+    return lax.cond(pairs < (DEPTH + 1) ** 2, sparse, dense, amplitudes, flat_int, mask, tile_irrep)
 
 
 def solution(mesh):

time: 74.6 us -> 71.6 us (0.960)
  Pallas kernels: 71.5 us -> 68.5 us
    pallas_call x1, Pallas kernels: 71.5 us -> 68.5 us  [sparse(): pl.pallas_call(sparse_kernel, out_shape=jax.ShapeDtypeStruct((2, 8, NO, V...]
where the time goes in v3:
time: 71.6 us; the launch traced here: 71.4 us
  Pallas kernels  68.5 us (96%)
  local copies, waits for them, and re-layouts  1.45 us (2%)
    pallas_call x1, Pallas kernels, sparse(): pl.pallas_call(sparse_kernel, out_shape=jax.ShapeDtypeStruct((2, 8, NO, V...  68.5 us
    unnamed x3, local copies, waits for them, and re-layouts  1.45 us

profile of v3, /device:TPU:1, one launch (start us, length us, event | category | flops | bytes accessed | tf_op | source)
XLA Modules:
  0.0 71.4 jit_solution(9728293729780302127)
XLA Ops:
  0.0 0.0 copy-start
  0.0 0.7 copy-done
  0.7 0.7 convert_reduce_fusion
  2.0 68.6 %conditional.1 = (f32[2,8,32,256]{3,2,1,0:T(8,128)S(1)}) conditional(s32[]{:T(128)} %convert_element_type.7, (f32[2,16,8,256]{3,2,1,0:T(8,128)}, f32[16,16,8,32]{3,2,1,0:T(8,128)}, s32[2,4,4,16]{3,2,1,0:T(4,128)}, s32[36]{0:T(128)S(1)}) %tuple.20, (f32[2,16,8,256]{3,2,1,0:T(8,128)}, f32[16,16,8,32]{3,2,1,0:T(8,128)}, s32[2,4,4,16]{3,2,1,0:T(4,128)}, ...), branch_computations={%region_1.0_spmd, %region_2.0_spmd} | conditional | bytes 8 | solution.py:642
  2.0 68.5 %branch_1_fun.1 = f32[2,8,32,256]{3,2,1,0:T(8,128)S(1)} custom-call(f32[2,16,8,256]{3,2,1,0:T(8,128)} %get-tuple-element.38.amp_hbm, f32[2048,32]{1,0:T(8,128)} %bitcast.8, s32[2,4,4,16]{3,2,1,0:T(4,128)} %get-tuple-element.30.mask_ref, s32[36]{0:T(128)S(1)} %get-tuple-element.31.irrep_ref), custom_call_target="tpu_custom_call" | custom-call | tf_op jit(solution)/shard_map/cond/branch_1_fun/pallas_call | solution.py:609
  70.6 0.8 %copy.12 = f32[2,8,32,256]{3,2,1,0:T(8,128)} copy(f32[2,8,32,256]{3,2,1,0:T(8,128)S(1)} %get-tuple-element.32) | data formatting | bytes 1048576
Async XLA Ops:
  0.0 0.7 copy-start

commit v4 on v3

--- a/solution.py
+++ b/solution.py
@@ -425,11 +425,11 @@
             lax.fori_loop(0, 8, one, 0)
             high_all[o], low_all[o] = split(wide[...])
 
-    def contract(i, dx, start=False):
+    def contract(i, dx, start=False, first=-1, count=4):
         base = ((x + dx + 4) % 4) * 4
 
         def one(step, carry):
-            o = base + step
+            o = base + (yh + first + step + 4) % 4
             high = high_all[o]
             left_side = jnp.concatenate([high, high, low_all[o]], axis=1)
             piece = jnp.concatenate([amp_all[i, 2 * o][:, None], amp_all[i, 2 * o + 1][:, None]], axis=1).reshape(V, V)
@@ -438,11 +438,11 @@
             acc[i] += jnp.dot(left_side, right_side, preferred_element_type=F32)
             return carry
 
-        for dy in (0, -1, 1, 2):
+        for dy in range(first, first + count):
             share_wait[i, dx, dy]()
         if start:
             acc[i] = jnp.zeros((V, V), F32)
-        lax.fori_loop(0, 4, one, 0)
+        lax.fori_loop(0, count, one, 0)
 
     passed = []
 
@@ -514,6 +514,7 @@
     x_forward(0, 0)
     z_forward(0, 1, 1)
     z_forward(0, 2, 0)
+    x_forward(1, 0)
     y_forward(0)
     y_start(1)
     z_forward(0, 2, 1)
@@ -532,7 +533,6 @@
     x_forward(0, 1)
     z_forward(1, 2, 0)
     unpack((3, 0), (-3, 0), (4, 0), (0, 1))
-    x_forward(1, 0)
     z_forward(1, 2, 1)
     y_forward(1)
     z_forward(1, 3, 0)
@@ -549,20 +549,21 @@
     y_end(1)
     x_end(0, 2)
     contract(0, 1)
+    x_forward(1, -1)
     contract(0, -1)
-    x_forward(1, -1)
     contract(0, 2)
+    x_forward(1, 1)
     exchange(0)
+    x_forward(1, 2)
     x_end(1, 0)
-    x_forward(1, 1)
     contract(1, 0, True)
-    x_forward(1, 2)
     x_end(1, -1)
     contract(1, 1)
     x_end(1, 1)
     contract(1, -1)
+    contract(1, 2, first=-1, count=3)
     x_end(1, 2)
-    contract(1, 2)
+    contract(1, 2, first=2, count=1)
     exchange(1)
     for copy in sent:
         copy.wait_send()

time: 71.6 us -> 70.6 us (0.986)
  Pallas kernels: 68.5 us -> 67.5 us
    pallas_call x1, Pallas kernels: 68.5 us -> 67.5 us  [sparse(): pl.pallas_call(sparse_kernel, out_shape=jax.ShapeDtypeStruct((2, 8, NO, V...]
where the time goes in v4:
time: 70.6 us; the launch traced here: 70.4 us
  Pallas kernels  67.5 us (96%)
  local copies, waits for them, and re-layouts  1.45 us (2%)
    pallas_call x1, Pallas kernels, sparse(): pl.pallas_call(sparse_kernel, out_shape=jax.ShapeDtypeStruct((2, 8, NO, V...  67.5 us
    unnamed x3, local copies, waits for them, and re-layouts  1.45 us

profile of v4, /device:TPU:1, one launch (start us, length us, event | category | flops | bytes accessed | tf_op | source)
XLA Modules:
  0.0 70.4 jit_solution(14514078889056626761)
XLA Ops:
  0.0 0.0 copy-start
  0.0 0.7 copy-done
  0.7 0.7 convert_reduce_fusion
  2.0 67.5 %conditional.1 = (f32[2,8,32,256]{3,2,1,0:T(8,128)S(1)}) conditional(s32[]{:T(128)} %convert_element_type.7, (f32[2,16,8,256]{3,2,1,0:T(8,128)}, f32[16,16,8,32]{3,2,1,0:T(8,128)}, s32[2,4,4,16]{3,2,1,0:T(4,128)}, s32[36]{0:T(128)S(1)}) %tuple.20, (f32[2,16,8,256]{3,2,1,0:T(8,128)}, f32[16,16,8,32]{3,2,1,0:T(8,128)}, s32[2,4,4,16]{3,2,1,0:T(4,128)}, ...), branch_computations={%region_1.0_spmd, %region_2.0_spmd} | conditional | bytes 8 | solution.py:643
  2.0 67.5 %branch_1_fun.1 = f32[2,8,32,256]{3,2,1,0:T(8,128)S(1)} custom-call(f32[2,16,8,256]{3,2,1,0:T(8,128)} %get-tuple-element.38.amp_hbm, f32[2048,32]{1,0:T(8,128)} %bitcast.8, s32[2,4,4,16]{3,2,1,0:T(4,128)} %get-tuple-element.30.mask_ref, s32[36]{0:T(128)S(1)} %get-tuple-element.31.irrep_ref), custom_call_target="tpu_custom_call" | custom-call | tf_op jit(solution)/shard_map/cond/branch_1_fun/pallas_call | solution.py:610
  69.6 0.8 %copy.12 = f32[2,8,32,256]{3,2,1,0:T(8,128)} copy(f32[2,8,32,256]{3,2,1,0:T(8,128)S(1)} %get-tuple-element.32) | data formatting | bytes 1048576
Async XLA Ops:
  0.0 0.7 copy-start

commit v5 on v4

--- a/solution.py
+++ b/solution.py
@@ -290,12 +290,13 @@
 
     spread = (lax.broadcasted_iota(jnp.int32, (4, V), 1) // TILE == lax.broadcasted_iota(jnp.int32, (4, V), 0)).astype(F32)
     load_amp.wait()
-    for i in range(2):
+    def mask(i):
         kept = lax.dot_general(
             mask_ref[i, vir // 8].astype(F32), spread, (((0,), (0,)), ((), ())), preferred_element_type=F32
         )
         amp_all[i, vir] = amp_in[i] * kept[:, None, :]
 
+    mask(0)
     pl.semaphore_wait(barrier, 20)
 
     count = [0]
@@ -476,6 +477,7 @@
 
     y_start(0)
     x_start(0, 0)
+    mask(1)
     x_start(1, 0)
 
     lane = lax.broadcasted_iota(jnp.int32, (NO, V), 1) // 16

time: 70.6 us -> 70.8 us (level)
  no operation moved by 1% of the time
where the time goes in v5:
time: 70.8 us; the launch traced here: 70.6 us
  Pallas kernels  67.8 us (96%)
  local copies, waits for them, and re-layouts  1.45 us (2%)
    pallas_call x1, Pallas kernels, sparse(): pl.pallas_call(sparse_kernel, out_shape=jax.ShapeDtypeStruct((2, 8, NO, V...  67.8 us
    unnamed x3, local copies, waits for them, and re-layouts  1.45 us

profile of v5, /device:TPU:1, one launch (start us, length us, event | category | flops | bytes accessed | tf_op | source)
XLA Modules:
  0.0 70.6 jit_solution(15559206176172639119)
XLA Ops:
  0.0 0.0 copy-start
  0.0 0.7 copy-done
  0.7 0.7 convert_reduce_fusion
  2.0 67.8 %conditional.1 = (f32[2,8,32,256]{3,2,1,0:T(8,128)S(1)}) conditional(s32[]{:T(128)} %convert_element_type.7, (f32[2,16,8,256]{3,2,1,0:T(8,128)}, f32[16,16,8,32]{3,2,1,0:T(8,128)}, s32[2,4,4,16]{3,2,1,0:T(4,128)}, s32[36]{0:T(128)S(1)}) %tuple.20, (f32[2,16,8,256]{3,2,1,0:T(8,128)}, f32[16,16,8,32]{3,2,1,0:T(8,128)}, s32[2,4,4,16]{3,2,1,0:T(4,128)}, ...), branch_computations={%region_1.0_spmd, %region_2.0_spmd} | conditional | bytes 8 | solution.py:645
  2.0 67.8 %branch_1_fun.1 = f32[2,8,32,256]{3,2,1,0:T(8,128)S(1)} custom-call(f32[2,16,8,256]{3,2,1,0:T(8,128)} %get-tuple-element.38.amp_hbm, f32[2048,32]{1,0:T(8,128)} %bitcast.8, s32[2,4,4,16]{3,2,1,0:T(4,128)} %get-tuple-element.30.mask_ref, s32[36]{0:T(128)S(1)} %get-tuple-element.31.irrep_ref), custom_call_target="tpu_custom_call" | custom-call | tf_op jit(solution)/shard_map/cond/branch_1_fun/pallas_call | solution.py:612
  69.8 0.8 %copy.12 = f32[2,8,32,256]{3,2,1,0:T(8,128)} copy(f32[2,8,32,256]{3,2,1,0:T(8,128)S(1)} %get-tuple-element.32) | data formatting | bytes 1048576
Async XLA Ops:
  0.0 0.7 copy-start
